TPU v7x, 256 devices: a whole 4x4x8 slice. The times are simulated.
256 devices in a mesh: dp: 32 (over x, z), tensor: 8 (over y, core).
Axes of the slice: x: 4, y: 4, z: 8, core: 2. Of those that a mesh axis runs over, the one named last changes fastest.
Arguments:
- activations: bfloat16 [2048, 24, 14336], P('dp', None, 'tensor'), may hold values from -6 to 6
- out_grads: bfloat16 [2048, 24, 4096], P('dp', None, 'tensor'), may hold values from -6 to 6
- proj_in: bfloat16 [14336, 64], P('tensor'), may hold values from -0.046875 to 0.046875
- proj_out: bfloat16 [4096, 64], P('tensor'), may hold values from -0.09375 to 0.09375
- queries: bfloat16 [32, 5120, 4096], P('dp', 'tensor'), may hold values from -0.09375 to 0.09375
- candidates: int32 [2048, 4], P('dp'), may hold values from 0 to 31, all different within a row; in each aligned block of 64 rows (0 to 63, 64 to 127, ...) at most 20 rows name the same one
Outputs:
- scores: float32 [2048, 4, 5120], P('dp', None, 'tensor')
Inputs may be any that keep to these rules, and one draw needn't show every extreme that they name: `candidates`: each example names 4 different groups. Among the 64 examples of one index of dp at most 20 name the same group, and in every draw some group is named by exactly 20 of them.
All inputs are finite; a program needn't handle non-finite values.
Results may differ from a plain program's by a relative error of at most 0.0029.
Values may be sent and summed in bfloat16 or wider, within the bound.
A program may use at most 64 MiB of HBM per device.

v0:
```python
import jax
import jax.numpy as jnp
from jax import lax
from jax.sharding import PartitionSpec as P

epsilon = 1e-06


def local(activations, out_grads, proj_in, proj_out, queries, candidates):
    examples_here, tokens_here, hidden_here = activations.shape
    proj_rank = proj_in.shape[1]
    per_example = candidates.shape[1]
    groups = lax.axis_size("dp")
    capacity = max(2, 5 * examples_here * per_example // (2 * groups))
    act_proj = jnp.dot(
        activations.reshape(examples_here * tokens_here, hidden_here),
        proj_in,
        preferred_element_type=jnp.float32,
    )
    grad_proj = jnp.dot(
        out_grads.reshape(examples_here * tokens_here, out_grads.shape[2]),
        proj_out,
        preferred_element_type=jnp.float32,
    )
    both_proj = jnp.concatenate([grad_proj, act_proj], axis=1).reshape(
        examples_here, tokens_here, 2 * proj_rank
    )
    summed = lax.psum(both_proj, "tensor")
    grad_side = summed[:, :, :proj_rank]
    act_side = summed[:, :, proj_rank:]
    example_grads = jnp.einsum(
        "eta,etb->eab", grad_side, act_side, precision=lax.Precision.HIGHEST
    ).reshape(examples_here, proj_rank * proj_rank)
    inv_rms = lax.rsqrt(jnp.mean(example_grads * example_grads, axis=1, keepdims=True) + epsilon)
    unit_grads = (example_grads * inv_rms).astype(jnp.bfloat16)
    flat_cands = candidates.reshape(-1)
    hit_table = (flat_cands[:, None] == jnp.arange(groups, dtype=jnp.int32)[None, :]).astype(
        jnp.int32
    )
    earlier = jnp.cumsum(hit_table, axis=0) - hit_table
    slot_index = jnp.sum(earlier * hit_table, axis=1)
    dest_index = flat_cands * capacity + slot_index
    row_copies = jnp.repeat(unit_grads, per_example, axis=0)
    grad_width = unit_grads.shape[1]
    send_buffer = (
        jnp.zeros((groups * capacity, grad_width), jnp.bfloat16).at[dest_index].set(row_copies)
    )
    send_buffer = send_buffer.reshape(groups, capacity, grad_width)
    query_block = queries[0]
    slot_scores = jnp.einsum(
        "gsk,qk->gsq",
        lax.all_to_all(send_buffer, "dp", split_axis=0, concat_axis=0, tiled=True),
        query_block,
        preferred_element_type=jnp.float32,
    )
    returned = lax.all_to_all(slot_scores, "dp", split_axis=0, concat_axis=0, tiled=True)
    picked = returned.reshape(groups * capacity, returned.shape[2])[dest_index]
    return picked.reshape(examples_here, per_example, returned.shape[2])


def solution(mesh):
    placed = (
        P("dp", None, "tensor"),
        P("dp", None, "tensor"),
        P("tensor", None),
        P("tensor", None),
        P("dp", "tensor", None),
        P("dp", None),
    )
    return jax.shard_map(
        local, mesh=mesh, in_specs=placed, out_specs=P("dp", None, "tensor"), check_vma=False
    )
```

profile of v0, /device:TPU:24, one launch (start us, length us, event | category | flops | bytes accessed | tf_op | source)
XLA Modules:
  0.0 337.4 jit_solution(5751738510498375177)
XLA Ops:
  6.5 0.0 copy-start
  6.5 0.0 all-reduce.2.cloned.1.call-start
  6.5 1.4 copy-done
  7.9 1.4 fusion.11
  9.4 0.0 copy-start.1
  9.4 4.3 %fusion.12 = f32[1536,64]{0,1:T(8,128)S(1)} fusion(bf16[1536,1792]{1,0:T(8,128)(2,1)} %bitcast.34, bf16[1792,64]{0,1:T(8,128)(2,1)} %param.8), kind=kOutput, calls=%fused_computation.26 | convolution fusion | flops 352321536 | bytes 6127616 | tf_op jit(solution)/shard_map/dot_general | solution.py:15
  13.7 0.1 pad_maximum_fusion
  13.8 1.1 copy.19
  14.9 0.0 all-reduce.2.cloned.1.call-update
  15.0 0.0 copy-done.1
  15.0 0.1 copy.16
  15.1 0.1 eq.29
  15.2 0.6 reduce-window.6
  15.8 0.2 slice_reduce_fusion
  16.0 0.1 eq.25
  16.1 0.1 copy.15
  16.2 0.1 mul.33
  16.3 0.1 fusion.9
  16.4 66.1 %all-reduce.2.cloned.1.call-done = f32[64,24,128]{2,1,0:T(8,128)} async-done(((f32[64,24,128]{2,1,0:T(8,128)}), f32[64,24,128]{2,1,0:T(8,128)}) %all-reduce.2.cloned.1.call-update) | async-done | bytes 786448 | tf_op jit(solution)/shard_map/psum | solution.py:28
  82.6 7.0 %multiply_reduce_fusion = (f32[64]{0:T(128)S(1)}, f32[64,64,64]{2,1,0:T(8,128)}) fusion(f32[64,24,128]{2,1,0:T(8,128)} %all-reduce.2.cloned.1.call-done), kind=kOutput, calls=%fused_computation.6 | convolution fusion | flops 76021696 | bytes 2621696 | tf_op jit(solution)/shard_map/eta,etb->eab/dot_general | solution.py:31
  89.5 2.1 reshape.82
  91.7 0.1 multiply_convert_fusion
  91.8 2.3 broadcast_in_dim.5
  94.1 4.0 %reshape.99 = bf16[256,4096]{1,0:T(8,128)(2,1)} reshape(bf16[64,4,4096]{2,1,0:T(4,128)(2,1)} %broadcast_in_dim.5) | data formatting | bytes 4194304 | tf_op jit(solution)/shard_map/reshape | solution.py:43
  98.1 7.7 %scatter_custom_fusion = bf16[640,4096]{1,0:T(8,128)(2,1)} fusion(s32[256]{0:T(256)S(1)} %bitcast.36, bf16[256,4096]{1,0:T(8,128)(2,1)} %reshape.99, bf16[]{:T(256)} %constant.7.clone.1), kind=kCustom, calls=%fused_computation.4 | custom fusion | bytes 5243392 | tf_op jit(solution)/shard_map/scatter | solution.py:46
  105.8 0.0 slice-start
  105.8 7.8 %reshape.84 = bf16[32,20,4096]{2,1,0:T(8,128)(2,1)} reshape(bf16[640,4096]{1,0:T(8,128)(2,1)} %scatter_custom_fusion) | data formatting | bytes 10485760 | tf_op jit(solution)/shard_map/reshape | solution.py:48
  113.6 0.0 slice-start.1
  113.6 151.8 %all_to_all.10 = bf16[32,20,4096]{2,1,0:T(8,128)(2,1)S(1)} all-to-all(bf16[32,20,4096]{2,1,0:T(8,128)(2,1)} %reshape.84), channel_id=1, replica_groups=mesh['dp'=32,'tensor'=8] {'dp'}, dimensions={0} | all-to-all | bytes 10485760 | tf_op jit(solution)/shard_map/all_to_all | solution.py:52
  265.4 0.0 slice-done
  265.4 0.0 slice-done.1
  265.4 6.5 %fusion = f32[32,20,640]{2,1,0:T(8,128)} fusion(bf16[32,20,4096]{2,1,0:T(8,128)(2,1)S(1)} %all_to_all.10, bf16[1,640,4096]{2,1,0:T(8,128)(2,1)S(1)} %bitcast.40), kind=kOutput, calls=%fused_computation.2 | convolution fusion | flops 3355443200 | bytes 12124160 | tf_op jit(solution)/shard_map/gsk,qk->gsq/dot_general | solution.py:50
  271.9 5.5 %all-to-all-start.1 = ((f32[32,20,640]{2,1,0:T(8,128)}), f32[32,20,640]{2,1,0:T(8,128)}, u32[]{:S(2)}, u32[]{:S(2)}) async-start(f32[32,20,640]{2,1,0:T(8,128)} %fusion), calls=%async_computation.1 | async-start | bytes 3932160 | tf_op jit(solution)/shard_map/all_to_all | solution.py:56
  277.4 47.6 %all-to-all-done.1 = f32[32,20,640]{2,1,0:T(8,128)} async-done(((f32[32,20,640]{2,1,0:T(8,128)}), f32[32,20,640]{2,1,0:T(8,128)}, u32[]{:S(2)}, u32[]{:S(2)}) %all-to-all-start.1) | async-done | bytes 1638432 | tf_op jit(solution)/shard_map/all_to_all | solution.py:56
  325.0 1.6 reshape.85
  326.6 1.9 gather_fusion
  328.5 2.1 reshape.86
  (8 shorter events, 0.1 us)
Async XLA Ops:
  6.5 1.4 copy-start
  6.5 76.0 %all-reduce.2.cloned.1.call-start = ((), (), s32[]{:S(2)}) async-start(), calls=%async_computation.2 | async-start | bytes 1572864 | tf_op jit(solution)/shard_map/psum | solution.py:28
  9.4 5.6 %copy-start.1 = (s32[64,4]{0,1:T(4,128)S(1)}, s32[64,4]{0,1:T(4,128)}, u32[]{:S(2)}) copy-start(s32[64,4]{0,1:T(4,128)} %param.11) | copy-start | bytes 3076
  105.8 159.6 %slice-start = ((s8[5242880]{0:T(1024)(128)(4,1)}), s8[1048576]{0:T(1024)(128)(4,1)S(1)}, s32[]{:S(2)}) async-start(s8[5242880]{0:T(1024)(128)(4,1)} %bitcast.39), calls=%async_computation.3 | async-start | bytes 2097152
  113.6 151.8 %slice-start.1 = ((s8[5242880]{0:T(1024)(128)(4,1)}), s8[4194304]{0:T(1024)(128)(4,1)S(1)}, s32[]{:S(2)}) async-start(s8[5242880]{0:T(1024)(128)(4,1)} %bitcast.39), calls=%async_computation.4 | async-start | bytes 8388608
  271.9 53.1 %all-to-all-start.1 = ((f32[32,20,640]{2,1,0:T(8,128)}), f32[32,20,640]{2,1,0:T(8,128)}, u32[]{:S(2)}, u32[]{:S(2)}) async-start(f32[32,20,640]{2,1,0:T(8,128)} %fusion), calls=%async_computation.1 | async-start | bytes 3932160 | tf_op jit(solution)/shard_map/all_to_all | solution.py:56
Sparse Core Ops, SparseCore 0:
  15.1 67.4 all-reduce.1
where the time goes:
time: 338 us; the launch traced here: 337 us
  blocking collectives  152 us (45%)
  waiting for transfers between devices  114 us (34%)
  local copies, waits for them, and re-layouts  32.8 us (10%)
  matrix products  19.2 us (6%)
  between operations  13.5 us (4%)
  starting transfers between devices  5.54 us (2%)
    all_to_all x1, blocking collectives, local(): lax.all_to_all(send_buffer, 'dp', split_axis=0, concat_axis=0, tiled=True)  152 us
    psum x1, waiting for transfers between devices, local(): summed = lax.psum(both_proj, 'tensor')  66.1 us
    all_to_all x1, waiting for transfers between devices, local(): lax.all_to_all(slot_scores, 'dp', split_axis=0, concat_axis=0, tiled=True)  47.6 us
    reshape x1, local copies, waits for them, and re-layouts, local(): send_buffer = send_buffer.reshape(groups, capacity, grad_width)  7.78 us
    scatter x1, local copies, waits for them, and re-layouts, local(): jnp.zeros((groups * capacity, grad_width), jnp.bfloat16).at[dest_index]  7.75 us
    dot_general x1, matrix products, local(): jnp.einsum('eta,etb->eab', grad_side, act_side, precision=lax.Precision.H...  6.96 us
  transfers between devices with their start and end apart: 2, of which 2 were waited for; matrix products, arithmetic and copies ran while one was open for 0% of the time, Pallas kernels for 0%

commit v1 on v0

--- a/solution.py
+++ b/solution.py
@@ -25,7 +25,7 @@
     both_proj = jnp.concatenate([grad_proj, act_proj], axis=1).reshape(
         examples_here, tokens_here, 2 * proj_rank
     )
-    summed = lax.psum(both_proj, "tensor")
+    summed = lax.all_gather(both_proj, "tensor").sum(axis=0)
     grad_side = summed[:, :, :proj_rank]
     act_side = summed[:, :, proj_rank:]
     example_grads = jnp.einsum(

time: 338 us -> 317 us (0.938)
  waiting for transfers between devices: 114 us -> 89.9 us
    psum x1 -> x0, waiting for transfers between devices: 66.1 us -> none  [local(): summed = lax.psum(both_proj, 'tensor')]
    all_gather x0 -> x1, waiting for transfers between devices: none -> 42.9 us  [local(): summed = lax.all_gather(both_proj, 'tensor').sum(axis=0)]
where the time goes in v1:
time: 317 us; the launch traced here: 315 us
  blocking collectives  151 us (48%)
  waiting for transfers between devices  89.9 us (28%)
  local copies, waits for them, and re-layouts  32.8 us (10%)
  matrix products  17.8 us (6%)
  between operations  13.5 us (4%)
  starting transfers between devices  5.22 us (2%)
  other arithmetic  4.11 us (1%)
    all_to_all x1, blocking collectives, local(): lax.all_to_all(send_buffer, 'dp', split_axis=0, concat_axis=0, tiled=True)  151 us
    all_to_all x1, waiting for transfers between devices, local(): lax.all_to_all(slot_scores, 'dp', split_axis=0, concat_axis=0, tiled=True)  47 us
    all_gather x1, waiting for transfers between devices, local(): summed = lax.all_gather(both_proj, 'tensor').sum(axis=0)  42.9 us
    reshape x1, local copies, waits for them, and re-layouts, local(): send_buffer = send_buffer.reshape(groups, capacity, grad_width)  7.78 us
    scatter x1, local copies, waits for them, and re-layouts, local(): jnp.zeros((groups * capacity, grad_width), jnp.bfloat16).at[dest_index]  7.75 us
    dot_general x1, matrix products, local(): jnp.einsum('gsk,qk->gsq', lax.all_to_all(send_buffer, 'dp', split_axis=0,...  6.46 us
  transfers between devices with their start and end apart: 2, of which 2 were waited for; matrix products, arithmetic and copies ran while one was open for 0% of the time, Pallas kernels for 0%

profile of v1, /device:TPU:24, one launch (start us, length us, event | category | flops | bytes accessed | tf_op | source)
XLA Modules:
  0.0 314.8 jit_solution(15812162282688348709)
XLA Ops:
  6.5 0.0 copy-start
  6.5 0.0 all-gather.2.cloned.1.call-start
  6.5 1.4 copy-done
  7.9 1.4 fusion.11
  9.4 0.0 copy-start.1
  9.4 4.3 %fusion.12 = f32[1536,64]{0,1:T(8,128)S(1)} fusion(bf16[1536,1792]{1,0:T(8,128)(2,1)} %bitcast.34, bf16[1792,64]{0,1:T(8,128)(2,1)} %param.8), kind=kOutput, calls=%fused_computation.26 | convolution fusion | flops 352321536 | bytes 6127616 | tf_op jit(solution)/shard_map/dot_general | solution.py:15
  13.7 0.1 pad_maximum_fusion
  13.8 1.2 copy.18
  14.9 0.0 all-gather.2.cloned.1.call-update
  15.0 0.0 copy-done.1
  15.0 0.1 copy.15
  15.1 0.1 eq.29
  15.2 0.1 eq.25
  15.3 0.6 reduce-window.6
  15.9 0.2 slice_reduce_fusion
  16.1 0.1 copy.14
  16.2 0.1 mul.33
  16.3 0.1 fusion.9
  16.4 42.9 %all-gather.2.cloned.1.call-done = f32[8,64,24,128]{3,2,1,0:T(8,128)} async-done(((f32[1,64,24,128]{3,2,1,0:T(8,128)}), f32[8,64,24,128]{3,2,1,0:T(8,128)}) %all-gather.2.cloned.1.call-update) | async-done | bytes 6291472 | tf_op jit(solution)/shard_map/all_gather | solution.py:28
  59.3 3.2 %reduce_sum.31 = f32[64,24,128]{2,1,0:T(8,128)S(1)} reduce(f32[8,64,24,128]{3,2,1,0:T(8,128)} %all-gather.2.cloned.1.call-done, f32[]{:T(128)} %constant.6.clone.1), dimensions={0}, to_apply=%region_3.4 | reduce | flops 1376256 | bytes 7077892 | tf_op jit(solution)/shard_map/reduce_sum | solution.py:28
  62.5 5.6 %multiply_reduce_fusion = (f32[64]{0:T(128)S(1)}, f32[64,64,64]{2,1,0:T(8,128)}) fusion(f32[64,24,128]{2,1,0:T(8,128)S(1)} %reduce_sum.31), kind=kOutput, calls=%fused_computation.6 | convolution fusion | flops 76021696 | bytes 2621696 | tf_op jit(solution)/shard_map/eta,etb->eab/dot_general | solution.py:31
  68.1 2.1 reshape.78
  70.2 0.1 multiply_convert_fusion
  70.4 2.3 broadcast_in_dim.5
  72.7 4.0 %reshape.95 = bf16[256,4096]{1,0:T(8,128)(2,1)} reshape(bf16[64,4,4096]{2,1,0:T(4,128)(2,1)} %broadcast_in_dim.5) | data formatting | bytes 4194304 | tf_op jit(solution)/shard_map/reshape | solution.py:43
  76.7 7.7 %scatter_custom_fusion = bf16[640,4096]{1,0:T(8,128)(2,1)} fusion(s32[256]{0:T(256)S(1)} %bitcast.36, bf16[256,4096]{1,0:T(8,128)(2,1)} %reshape.95, bf16[]{:T(256)} %constant.7.clone.1), kind=kCustom, calls=%fused_computation.4 | custom fusion | bytes 5243392 | tf_op jit(solution)/shard_map/scatter | solution.py:46
  84.4 0.0 slice-start
  84.4 7.8 %reshape.80 = bf16[32,20,4096]{2,1,0:T(8,128)(2,1)} reshape(bf16[640,4096]{1,0:T(8,128)(2,1)} %scatter_custom_fusion) | data formatting | bytes 10485760 | tf_op jit(solution)/shard_map/reshape | solution.py:48
  92.2 0.0 slice-start.1
  92.2 151.4 %all_to_all.10 = bf16[32,20,4096]{2,1,0:T(8,128)(2,1)S(1)} all-to-all(bf16[32,20,4096]{2,1,0:T(8,128)(2,1)} %reshape.80), channel_id=1, replica_groups=mesh['dp'=32,'tensor'=8] {'dp'}, dimensions={0} | all-to-all | bytes 10485760 | tf_op jit(solution)/shard_map/all_to_all | solution.py:52
  243.6 0.0 slice-done
  243.6 0.0 slice-done.1
  243.6 6.5 %fusion = f32[32,20,640]{2,1,0:T(8,128)} fusion(bf16[32,20,4096]{2,1,0:T(8,128)(2,1)S(1)} %all_to_all.10, bf16[1,640,4096]{2,1,0:T(8,128)(2,1)S(1)} %bitcast.40), kind=kOutput, calls=%fused_computation.2 | convolution fusion | flops 3355443200 | bytes 12124160 | tf_op jit(solution)/shard_map/gsk,qk->gsq/dot_general | solution.py:50
  250.1 5.2 %all-to-all-start.1 = ((f32[32,20,640]{2,1,0:T(8,128)}), f32[32,20,640]{2,1,0:T(8,128)}, u32[]{:S(2)}, u32[]{:S(2)}) async-start(f32[32,20,640]{2,1,0:T(8,128)} %fusion), calls=%async_computation.1 | async-start | bytes 3932160 | tf_op jit(solution)/shard_map/all_to_all | solution.py:56
  255.3 47.0 %all-to-all-done.1 = f32[32,20,640]{2,1,0:T(8,128)} async-done(((f32[32,20,640]{2,1,0:T(8,128)}), f32[32,20,640]{2,1,0:T(8,128)}, u32[]{:S(2)}, u32[]{:S(2)}) %all-to-all-start.1) | async-done | bytes 1638432 | tf_op jit(solution)/shard_map/all_to_all | solution.py:56
  302.3 1.6 reshape.81
  303.9 1.9 gather_fusion
  305.8 2.1 reshape.82
  (8 shorter events, 0.1 us)
Async XLA Ops:
  6.5 1.4 copy-start
  6.5 52.8 %all-gather.2.cloned.1.call-start = ((), (), s32[]{:S(2)}) async-start(), calls=%async_computation.2 | async-start | bytes 7077888 | tf_op jit(solution)/shard_map/all_gather | solution.py:28
  9.4 5.6 %copy-start.1 = (s32[64,4]{0,1:T(4,128)S(1)}, s32[64,4]{0,1:T(4,128)}, u32[]{:S(2)}) copy-start(s32[64,4]{0,1:T(4,128)} %param.11) | copy-start | bytes 3076
  84.4 159.2 %slice-start = ((s8[5242880]{0:T(1024)(128)(4,1)}), s8[1048576]{0:T(1024)(128)(4,1)S(1)}, s32[]{:S(2)}) async-start(s8[5242880]{0:T(1024)(128)(4,1)} %bitcast.39), calls=%async_computation.3 | async-start | bytes 2097152
  92.2 151.5 %slice-start.1 = ((s8[5242880]{0:T(1024)(128)(4,1)}), s8[4194304]{0:T(1024)(128)(4,1)S(1)}, s32[]{:S(2)}) async-start(s8[5242880]{0:T(1024)(128)(4,1)} %bitcast.39), calls=%async_computation.4 | async-start | bytes 8388608
  250.1 52.2 %all-to-all-start.1 = ((f32[32,20,640]{2,1,0:T(8,128)}), f32[32,20,640]{2,1,0:T(8,128)}, u32[]{:S(2)}, u32[]{:S(2)}) async-start(f32[32,20,640]{2,1,0:T(8,128)} %fusion), calls=%async_computation.1 | async-start | bytes 3932160 | tf_op jit(solution)/shard_map/all_to_all | solution.py:56
Sparse Core Ops, SparseCore 0:
  15.1 44.1 all-gather.1
